TPU v7x, 32 devices: a whole 2x2x4 slice. The times are simulated.
32 devices in a mesh: grp: 2 (over x), win: 4 (over z), seq: 4 (over y, core).
Axes of the slice: x: 2, y: 2, z: 4, core: 2. Of those that a mesh axis runs over, the one named last changes fastest.
Arguments:
- embeddings: bfloat16 [8, 768, 1536], P(('grp', 'win'), 'seq'), parts along dimension 0, may hold values from -48 to 48
- skip_rows: bfloat16 [8, 1536, 1536], P(('grp', 'win'), 'seq'), parts along dimension 0, may hold values from -6 to 6
- w_query: bfloat16 [1536, 256], replicated, may hold values from -0.16 to 0.16
- w_key: bfloat16 [1536, 256], replicated, may hold values from -10 to 10
- w_value: bfloat16 [1536, 768], replicated, may hold values from -0.15625 to 0.15625
- w_out: bfloat16 [768, 1536], replicated, may hold values from -0.21875 to 0.21875
- conv_taps: float32 [3, 1536], replicated, may hold values from -3 to 3
- w_head: bfloat16 [1536, 4096], P(None, 'seq'), may hold values from -0.15625 to 0.15625
- head_bias: float32 [4096], replicated, may hold values from -4 to 4
Outputs:
- genome_tracks: bfloat16 [8, 2, 4, 96, 4096], P(('grp', 'win'), None, 'seq'), parts along dimension 0
There are 2 independent parts, one for each index of `grp`. A program takes and returns all parts, laid end to end along the dimension named above; an argument that names none is the same for every part. Nothing has to cross between parts.
All inputs are finite; a program needn't handle non-finite values.
Results may differ from a plain program's by a relative error of at most 0.0075.
Values may be sent and summed in bfloat16 or wider, within the bound.
A program may use at most 128 MiB of HBM per device.

v0:
```python
import math

import jax
import jax.numpy as jnp
from jax import lax
from jax.sharding import PartitionSpec as P

HEADS = 4
KEY = 64
VAL = 192


def padded_2(cells, sides, width):
    for axis, dim in sides:
        count = lax.axis_size(axis)
        ends = count - 1
        head = lax.slice_in_dim(cells, 0, width, axis=dim)
        tail = lax.slice_in_dim(cells, cells.shape[dim] - width, cells.shape[dim], axis=dim)
        cells = jnp.concatenate(
            [
                lax.ppermute(tail, axis, [(i, (i + 1) % count) for i in range(ends)]),
                cells,
                lax.ppermute(head, axis, [((i + 1) % count, i) for i in range(ends)]),
            ],
            axis=dim,
        )
    return cells


def passed_along(value, axis, by):
    devices = lax.axis_size(axis)
    return lax.ppermute(value, axis, [(i, (i + by) % devices) for i in range(devices)])


def normalize(rows):
    centre = jnp.mean(rows, axis=-1, keepdims=True)
    centred = rows - centre
    spread = jnp.mean(centred * centred, axis=-1, keepdims=True)
    return centred * lax.rsqrt(spread + 1e-05)


def local(embeddings, skip_rows, w_query, w_key, w_value, w_out, conv_taps, w_head, head_bias):
    tok_count = embeddings.shape[1]
    seq_count = lax.axis_size("seq")
    piece_rows = 2 * tok_count // seq_count
    half_count = seq_count // 2
    window_len = seq_count * tok_count
    x_float = embeddings[0].astype(jnp.float32)
    normed = normalize(x_float).astype(jnp.bfloat16)
    query = (
        jnp.dot(normed, w_query, preferred_element_type=jnp.float32)
        .astype(jnp.bfloat16)
        .reshape(tok_count, HEADS, KEY)
    )
    key_rows = jnp.dot(normed, w_key, preferred_element_type=jnp.float32).astype(jnp.bfloat16)
    value_rows = jnp.dot(normed, w_value, preferred_element_type=jnp.float32).astype(jnp.bfloat16)
    run_max = jnp.full((tok_count, HEADS), -jnp.inf, jnp.float32)
    denom_sum = jnp.zeros((tok_count, HEADS), jnp.float32)
    acc_sum = jnp.zeros((tok_count, HEADS, VAL), jnp.float32)
    key_piece = lax.all_gather(key_rows, "seq", axis=0, tiled=True)
    val_piece = lax.all_gather(value_rows, "seq", axis=0, tiled=True)
    key_count = key_piece.shape[0]
    scores = jnp.einsum(
        "thk,nhk->thn",
        query,
        key_piece.reshape(key_count, HEADS, KEY),
        preferred_element_type=jnp.float32,
    ) / math.sqrt(KEY)
    new_max = jnp.max(scores, axis=-1)
    fade_by = jnp.exp(run_max - new_max)
    weights = jnp.exp(scores - new_max[..., None])
    denom_sum = denom_sum * fade_by + jnp.sum(weights, axis=-1)
    update = jnp.einsum(
        "thn,nhv->thv",
        weights.astype(jnp.bfloat16),
        val_piece.reshape(key_count, HEADS, VAL),
        preferred_element_type=jnp.float32,
    )
    acc_sum = acc_sum * fade_by[..., None] + update
    run_max, denom_sum, acc_sum = (new_max, denom_sum, acc_sum)
    attended = (acc_sum / denom_sum[..., None]).reshape(tok_count, HEADS * VAL).astype(jnp.bfloat16)
    resid = x_float + jnp.dot(attended, w_out, preferred_element_type=jnp.float32)
    upsampled = (jnp.repeat(resid, 2, axis=0) + skip_rows[0].astype(jnp.float32)).astype(
        jnp.bfloat16
    )
    padded = padded_2(upsampled, (("seq", 0),), 1).astype(jnp.float32)
    conv_out = conv_taps[0] * padded[:-2] + conv_taps[1] * padded[1:-1] + conv_taps[2] * padded[2:]
    features = jax.nn.gelu(conv_out, approximate=False).astype(jnp.bfloat16)
    received = lax.all_to_all(
        features.reshape(seq_count, piece_rows, -1), "seq", split_axis=0, concat_axis=0, tiled=True
    )
    behind_rows = passed_along(received[half_count:], "win", 1)
    both_rows = jnp.concatenate([received[:half_count], behind_rows], axis=0).reshape(
        2 * tok_count, -1
    )
    tracks = (
        jnp.dot(
            both_rows,
            lax.all_gather(w_head, "seq", axis=1, tiled=True),
            preferred_element_type=jnp.float32,
        )
        .astype(jnp.bfloat16)
        .reshape(seq_count, piece_rows, -1)
    )
    ahead_part = tracks[:half_count]
    behind = tracks[half_count:]
    seq_place = lax.axis_index("seq")
    offsets = (
        jnp.arange(half_count, dtype=jnp.int32)[:, None] * (2 * tok_count)
        + seq_place * piece_rows
        + jnp.arange(piece_rows, dtype=jnp.int32)[None, :]
    )
    offsets = offsets.astype(jnp.float32)[..., None]
    stitched = (
        (offsets + 1.0) * ahead_part.astype(jnp.float32)
        + (window_len - offsets) * behind.astype(jnp.float32)
    ) / (window_len + 1.0) + head_bias
    genome_tracks = jax.nn.softplus(stitched).astype(jnp.bfloat16)
    return genome_tracks[None, :, None]


def solution(mesh):
    return jax.shard_map(
        local,
        mesh=mesh,
        in_specs=(
            P(("grp", "win"), "seq", None),
            P(("grp", "win"), "seq", None),
            P(),
            P(),
            P(),
            P(),
            P(),
            P(None, "seq"),
            P(),
        ),
        out_specs=P(("grp", "win"), None, "seq", None, None),
        check_vma=False,
    )
```

profile of v0, /device:TPU:0, one launch (start us, length us, event | category | flops | bytes accessed | tf_op | source)
XLA Modules:
  0.0 148.8 jit_solution(15315957629014582520)
XLA Ops:
  6.5 1.4 convert_reduce_fusion
  7.9 1.4 fusion.26
  9.3 3.3 %convolution_convert_fusion.1 = bf16[192,768]{1,0:T(8,128)(2,1)} fusion(bf16[1536,768]{1,0:T(8,128)(2,1)} %param.13, bf16[1,192,1536]{2,1,0:T(8,128)(2,1)} %param.9, f32[192]{0:T(256)S(1)} %add_rsqrt_fusion, f32[192]{0:T(256)S(1)} %broadcast_multiply_fusion), kind=kOutput, calls=%fused_computation.49 | convolution fusion | flops 454311936 | bytes 3245568 | tf_op jit(solution)/shard_map/dot_general | solution.py:56
  13.7 1.5 %convolution_convert_fusion.3 = bf16[192,256]{1,0:T(8,128)(2,1)S(1)} fusion(bf16[1536,256]{1,0:T(8,128)(2,1)} %param.12, bf16[1,192,1536]{2,1,0:T(8,128)(2,1)S(1)} %copy-done.2, f32[192]{0:T(256)S(1)} %add_rsqrt_fusion, f32[192]{0:T(256)S(1)} %broadcast_multiply_fusion), kind=kOutput, calls=%fused_computation.57 | convolution fusion | flops 152223744 | bytes 1476096 | tf_op jit(solution)/shard_map/dot_general | solution.py:55
  15.2 8.0 %all_gather.9 = bf16[768,256]{1,0:T(8,128)(2,1)S(1)} all-gather(bf16[192,256]{1,0:T(8,128)(2,1)S(1)} %convolution_convert_fusion.3), channel_id=1, replica_groups=mesh['grp'=2,'win'=4,'seq'=4] {'seq'}, dimensions={0}, use_global_device_ids=true | all-gather | bytes 491520 | tf_op jit(solution)/shard_map/all_gather | solution.py:60
  24.0 2.2 %convolution_convert_fusion.2 = bf16[192,256]{1,0:T(8,128)(2,1)} fusion(bf16[1536,256]{1,0:T(8,128)(2,1)} %param.11, bf16[1,192,1536]{2,1,0:T(8,128)(2,1)S(1)} %copy-done.2, f32[192]{0:T(256)S(1)} %add_rsqrt_fusion, f32[192]{0:T(256)S(1)} %broadcast_multiply_fusion), kind=kOutput, calls=%fused_computation.56 | convolution fusion | flops 152223744 | bytes 1476096 | tf_op jit(solution)/shard_map/dot_general | solution.py:51
  27.9 1.4 copy-done.1
  29.9 3.0 %all-gather.3.cloned.1.call-done = bf16[768,768]{1,0:T(8,128)(2,1)} async-done(((bf16[192,768]{1,0:T(8,128)(2,1)}), bf16[768,768]{1,0:T(8,128)(2,1)}) %all-gather.3.cloned.1.call-update) | async-done | bytes 1179664 | tf_op jit(solution)/shard_map/all_gather | solution.py:61
  32.9 2.4 %copy.17 = bf16[768,768]{0,1:T(8,128)(2,1)} copy(bf16[768,768]{1,0:T(8,128)(2,1)} %all-gather.3.cloned.1.call-done) | data formatting | bytes 2359296 | tf_op jit(solution)/shard_map/all_gather | solution.py:61
  35.3 2.7 %fusion.25 = bf16[192,4,192]{0,2,1:T(8,128)(2,1)S(1)} fusion(bf16[768,4,192]{0,2,1:T(8,128)(2,1)} %bitcast.68, f32[4,768,192]{1,2,0:T(8,128)} %copy-done.1, f32[192,4]{0,1:T(4,128)S(1)} %get-tuple-element.18, f32[192,4]{0,1:T(4,128)S(1)} %get-tuple-element.15, f32[192,4]{0,1:T(4,128)S(1)} %get-tuple-element.14), kind=kOutput, calls=%fused_computation.48 | convolution fusion | flops 228704256 | bytes 3843072 | tf_op jit(solution)/shard_map/thn,nhv->thv/dot_general | solution.py:73
  38.7 2.2 %broadcast_in_dim.8 = f32[192,2,1536]{2,1,0:T(2,128)} broadcast(f32[192,1536]{1,0:T(8,128)S(1)} %convolution_add_fusion), dimensions={0,2} | broadcast | bytes 3538944 | tf_op jit(solution)/shard_map/broadcast_in_dim | solution.py:83
  41.0 4.3 %reshape.169 = f32[384,1536]{1,0:T(8,128)} reshape(f32[192,2,1536]{2,1,0:T(2,128)} %broadcast_in_dim.8) | data formatting | bytes 4718592 | tf_op jit(solution)/shard_map/reshape | solution.py:83
  45.3 2.2 %fusion.9 = bf16[384,1536]{1,0:T(8,128)(2,1)S(1)} fusion(f32[384,1536]{1,0:T(8,128)} %reshape.169, bf16[1,384,1536]{2,1,0:T(8,128)(2,1)S(1)} %copy-done.4), kind=kLoop, calls=%fused_computation.19 | loop fusion | flops 1769472 | bytes 4718592 | tf_op jit(solution)/shard_map/convert_element_type | solution.py:83
  47.5 2.2 %collective-permute-start = (bf16[1,1536]{1,0:T(2,128)(2,1)S(1)}, bf16[1,1536]{1,0:T(2,128)(2,1)S(1)}, u32[]{:S(2)}, u32[]{:S(2)}) collective-permute-start(bf16[1,1536]{1,0:T(2,128)(2,1)S(1)} %get-tuple-element.12), channel_id=1, source_target_pairs={{0,1},{1,2},{2,3},{4,5},{5,6},{6,7},{8,9},{9,10},{10,11},{12,13},{... | collective-permute-start | bytes 9224 | tf_op jit(solution)/shard_map/ppermute | solution.py:21
  49.7 1.3 collective-permute-start.1
  51.0 1.7 %collective-permute-done.1 = bf16[1,1536]{1,0:T(2,128)(2,1)S(1)} collective-permute-done((bf16[1,1536]{1,0:T(2,128)(2,1)S(1)}, bf16[1,1536]{1,0:T(2,128)(2,1)S(1)}, u32[]{:S(2)}, u32[]{:S(2)}) %collective-permute-start.1) | collective-permute-done | bytes 3104 | tf_op jit(solution)/shard_map/ppermute | solution.py:23
  53.1 5.9 %fusion.6 = bf16[384,1536]{1,0:T(8,128)(2,1)S(1)} fusion(f32[386,1536]{1,0:T(8,128)S(1)} %maximum_convert_fusion, f32[1536]{0:T(1024)S(1)} %get-tuple-element.6, f32[1536]{0:T(1024)S(1)} %get-tuple-element.7, f32[1536]{0:T(1024)S(1)} %get-tuple-element.5), kind=kLoop, calls=%fused_computation.12 | loop fusion | flops 41287680 | bytes 8275968 | tf_op jit(solution)/shard_map/convert_element_type | solution.py:88
  59.0 33.0 %all_to_all.5 = bf16[4,96,1536]{2,1,0:T(8,128)(2,1)S(1)} all-to-all(bf16[4,96,1536]{2,1,0:T(8,128)(2,1)S(1)} %bitcast.66), channel_id=1, replica_groups=mesh['grp'=2,'win'=4,'seq'=4] {'seq'}, dimensions={0} | all-to-all | bytes 2359296 | tf_op jit(solution)/shard_map/all_to_all | solution.py:89
  92.1 1.9 %collective-permute-start.2 = (bf16[2,96,1536]{2,1,0:T(8,128)(2,1)S(1)}, bf16[2,96,1536]{2,1,0:T(8,128)(2,1)}, u32[]{:S(2)}, u32[]{:S(2)}) collective-permute-start(bf16[2,96,1536]{2,1,0:T(8,128)(2,1)S(1)} %get-tuple-element.11), channel_id=1, source_target_pairs={{0,4},{4,8},{8,12},{12,0},{1,5},{5,9},{9,13},{13,1},{2,6},{6,10},{... | collective-permute-start | bytes 1769480 | tf_op jit(solution)/shard_map/ppermute | solution.py:32
  94.1 15.2 %collective-permute-done.2 = bf16[2,96,1536]{2,1,0:T(8,128)(2,1)} collective-permute-done((bf16[2,96,1536]{2,1,0:T(8,128)(2,1)S(1)}, bf16[2,96,1536]{2,1,0:T(8,128)(2,1)}, u32[]{:S(2)}, u32[]{:S(2)}) %collective-permute-start.2) | collective-permute-done | bytes 589856 | tf_op jit(solution)/shard_map/ppermute | solution.py:32
  109.2 2.2 %pad_maximum_fusion = bf16[4,96,1536]{2,1,0:T(8,128)(2,1)} fusion(bf16[2,96,1536]{2,1,0:T(8,128)(2,1)} %collective-permute-done.2, bf16[2,96,1536]{2,1,0:T(8,128)(2,1)S(1)} %get-tuple-element.10), kind=kLoop, calls=%fused_computation.53 | loop fusion | flops 589824 | bytes 2359296 | tf_op jit(solution)/shard_map/concatenate | solution.py:93
  111.4 17.9 %all-gather.5.cloned.1.call-done = bf16[1536,4096]{1,0:T(8,128)(2,1)} async-done(((bf16[1536,1024]{1,0:T(8,128)(2,1)}), bf16[1536,4096]{1,0:T(8,128)(2,1)}) %all-gather.5.cloned.1.call-update) | async-done | bytes 12582928 | tf_op jit(solution)/shard_map/all_gather | solution.py:99
  129.3 8.3 %convolution_convert_fusion = bf16[384,4096]{1,0:T(8,128)(2,1)S(1)} fusion(bf16[384,1536]{1,0:T(8,128)(2,1)} %bitcast.69, bf16[1536,4096]{1,0:T(8,128)(2,1)} %all-gather.5.cloned.1.call-done), kind=kOutput, calls=%fused_computation.1 | convolution fusion | flops 4833411072 | bytes 16908288 | tf_op jit(solution)/shard_map/dot_general | solution.py:97
  138.4 3.6 %fusion = bf16[1,2,1,96,4096]{4,3,2,1,0:T(8,128)(2,1)} fusion(bf16[1,2,1,96,4096]{4,3,2,1,0:T(8,128)(2,1)S(1)} %bitcast.65, bf16[1,2,1,96,4096]{4,3,2,1,0:T(8,128)(2,1)S(1)} %bitcast.64, f32[4096]{0:T(1024)S(1)} %copy-done.5, f32[2,96]{1,0:T(2,128)S(1)} %get-tuple-element.17, f32[2,96]{1,0:T(2,128)S(1)} %get-tuple-element.16), kind=kLoop, calls=%fused_computation.3 | loop fusion | flops 11010048 | bytes 4736512 | tf_op jit(solution)/shard_map/convert_element_type | solution.py:118
  (33 shorter events, 6.2 us)
Async XLA Ops:
  6.5 31.5 %copy-start = (bf16[768,1536]{1,0:T(8,128)(2,1)S(1)}, bf16[768,1536]{1,0:T(8,128)(2,1)}, u32[]{:S(2)}) copy-start(bf16[768,1536]{1,0:T(8,128)(2,1)} %param.14) | copy-start | bytes 7077892
  6.5 26.4 %all-gather.3.cloned.1.call-start = ((), (), s32[]{:S(2)}) async-start(), calls=%async_computation.1 | async-start | bytes 1474560 | tf_op jit(solution)/shard_map/all_gather | solution.py:61
  12.6 1.1 copy-start.2
  12.6 116.7 %all-gather.5.cloned.1.call-start = ((), (), s32[]{:S(2)}) async-start(), calls=%async_computation.2 | async-start | bytes 15728640 | tf_op jit(solution)/shard_map/all_gather | solution.py:99
  24.0 3.2 %copy-start.3 = (bf16[768,256]{0,1:T(8,128)(2,1)S(1)}, bf16[768,256]{0,1:T(8,128)(2,1)}, u32[]{:S(2)}) copy-start(bf16[768,256]{0,1:T(8,128)(2,1)} %copy.15) | copy-start | bytes 1179652
  27.9 1.4 copy-start.1
  41.0 4.3 %copy-start.4 = (bf16[1,384,1536]{2,1,0:T(8,128)(2,1)S(1)}, bf16[1,384,1536]{2,1,0:T(8,128)(2,1)}, u32[]{:S(2)}) copy-start(bf16[1,384,1536]{2,1,0:T(8,128)(2,1)} %param.10) | copy-start | bytes 3538948
  45.3 5.7 %copy-start.6 = (f32[3,1536]{1,0:T(4,128)S(1)}, f32[3,1536]{1,0:T(4,128)}, u32[]{:S(2)}) copy-start(f32[3,1536]{1,0:T(4,128)} %param.15) | copy-start | bytes 55300
  47.5 3.5 %collective-permute-start = (bf16[1,1536]{1,0:T(2,128)(2,1)S(1)}, bf16[1,1536]{1,0:T(2,128)(2,1)S(1)}, u32[]{:S(2)}, u32[]{:S(2)}) collective-permute-start(bf16[1,1536]{1,0:T(2,128)(2,1)S(1)} %get-tuple-element.12), channel_id=1, source_target_pairs={{0,1},{1,2},{2,3},{4,5},{5,6},{6,7},{8,9},{9,10},{10,11},{12,13},{... | collective-permute-start | bytes 9224 | tf_op jit(solution)/shard_map/ppermute | solution.py:21
  49.7 3.1 %collective-permute-start.1 = (bf16[1,1536]{1,0:T(2,128)(2,1)S(1)}, bf16[1,1536]{1,0:T(2,128)(2,1)S(1)}, u32[]{:S(2)}, u32[]{:S(2)}) collective-permute-start(bf16[1,1536]{1,0:T(2,128)(2,1)S(1)} %get-tuple-element.13), channel_id=1, source_target_pairs={{1,0},{2,1},{3,2},{5,4},{6,5},{7,6},{9,8},{10,9},{11,10},{13,12},{... | collective-permute-start | bytes 9224 | tf_op jit(solution)/shard_map/ppermute | solution.py:23
  92.1 17.1 %collective-permute-start.2 = (bf16[2,96,1536]{2,1,0:T(8,128)(2,1)S(1)}, bf16[2,96,1536]{2,1,0:T(8,128)(2,1)}, u32[]{:S(2)}, u32[]{:S(2)}) collective-permute-start(bf16[2,96,1536]{2,1,0:T(8,128)(2,1)S(1)} %get-tuple-element.11), channel_id=1, source_target_pairs={{0,4},{4,8},{8,12},{12,0},{1,5},{5,9},{9,13},{13,1},{2,6},{6,10},{... | collective-permute-start | bytes 1769480 | tf_op jit(solution)/shard_map/ppermute | solution.py:32
  137.6 0.7 copy-start.5
Sparse Core Ops, SparseCore 0:
  12.7 20.1 all-gather.2
  34.5 94.7 all-gather.4
where the time goes:
time: 149 us
  blocking collectives  41 us (28%)
  waiting for transfers between devices  38.5 us (26%)
  matrix products  19.4 us (13%)
  other arithmetic  17.6 us (12%)
  between operations  13.6 us (9%)
  local copies, waits for them, and re-layouts  13.4 us (9%)
  starting transfers between devices  5.41 us (4%)
    all_to_all x1, blocking collectives, local(): lax.all_to_all(features.reshape(seq_count, piece_rows, -1), 'seq', split_...  33 us
    all_gather x1, waiting for transfers between devices, local(): lax.all_gather(w_head, 'seq', axis=1, tiled=True)  17.9 us
    ppermute x1, waiting for transfers between devices, passed_along(): lax.ppermute(value, axis, [(i, (i + by) % devices) for i in range(devices)])  15.2 us
    dot_general x1, matrix products, local(): jnp.dot(both_rows, lax.all_gather(w_head, 'seq', axis=1, tiled=True), pre...  8.33 us
    all_gather x1, blocking collectives, local(): key_piece = lax.all_gather(key_rows, 'seq', axis=0, tiled=True)  7.95 us
    convert_element_type x1, other arithmetic, local(): features = jax.nn.gelu(conv_out, approximate=False).astype(jnp.bfloat16)  5.87 us
    reshape x1, local copies, waits for them, and re-layouts, local(): jnp.repeat(resid, 2, axis=0) + skip_rows[0].astype(jnp.float32)  4.29 us
    convert_element_type x1, other arithmetic, local(): genome_tracks = jax.nn.softplus(stitched).astype(jnp.bfloat16)  3.62 us
  transfers between devices with their start and end apart: 5, of which 4 were waited for; matrix products, arithmetic and copies ran while one was open for 20% of the time, Pallas kernels for 0%

commit v1 on v0

v1 whole, which is shorter than its diff:
```python
import functools
import math

import jax
import jax.numpy as jnp
from jax import lax
from jax.experimental import pallas as pl
from jax.experimental.pallas import tpu as pltpu
from jax.sharding import PartitionSpec as P

HEADS = 4
KEY = 64
VAL = 192
PAIRS = HEADS // 2
KP = 2 * KEY
VP = 2 * VAL
TILE = 256
MESH = pl.DeviceIdType.MESH


def normalize(rows):
    centre = jnp.mean(rows, axis=-1, keepdims=True)
    centred = rows - centre
    spread = jnp.mean(centred * centred, axis=-1, keepdims=True)
    return centred * lax.rsqrt(spread + 1e-05)


def gelu(x):
    return 0.5 * x * (1.0 + lax.erf(x * math.sqrt(0.5)))


def kernel(
    n, n_win, n_grp,
    emb_h, skip_h, wq_h, wk_h, wv_h, wo_h, taps_h, wh_h, bias_h, out_h,
    x_v, skip_v, wq_v, wk_v, wv_v, wo_v, taps_v, bias_v, wh_v,
    normed_v, q_v, kv_v, att_v, wide_v, even_v, odd_v, halo_s, halo_r,
    feat_v, got_v, blend_v, out_v,
    load_sem, send_sem, recv_sem, fsend_sem, frecv_sem, store_sem,
):
    grp = lax.axis_index("grp")
    win = lax.axis_index("win")
    seq = lax.axis_index("seq")
    tok, width = x_v.shape
    piece = feat_v.shape[1]
    cols = wh_v.shape[2]
    half = n // 2
    window_len = n * tok

    loads = {}
    for at, (name, src, dst) in enumerate(
        (
            ("x", emb_h.at[0], x_v),
            ("wk", wk_h, wk_v),
            ("wv", wv_h, wv_v),
            ("wq", wq_h, wq_v),
            ("skip", skip_h.at[0], skip_v),
            ("wo", wo_h, wo_v),
            ("taps", taps_h, taps_v),
            ("wh", wh_h, wh_v.at[seq]),
            ("bias", bias_h, bias_v),
        )
    ):
        loads[name] = pltpu.make_async_copy(src, dst, load_sem.at[at])
        loads[name].start()

    def dev(g, w, s):
        return (g, w, s)

    sibling = dev(grp, win, seq + 1 - 2 * (seq % 2))
    sib_seq = seq + 1 - 2 * (seq % 2)
    other_grp = 1 - grp
    other_win = win + 1 - 2 * (win % 2)
    across = dev(other_grp, win, seq)
    beside = dev(grp, other_win, seq)
    peers = [(seq + 2 * e) % n for e in range(1, half)]
    next_win = (win + 1) % n_win
    prev_win = (win + n_win - 1) % n_win

    barrier = pltpu.get_barrier_semaphore()
    greeted = [dev(grp, win, (seq + d) % n) for d in range(1, n)]
    greeted += [dev(grp, w, (seq + d) % n) for w in (next_win, prev_win) for d in range(n)]
    greeted.append(across)
    for target in greeted:
        pl.semaphore_signal(barrier, inc=1, device_id=target, device_id_type=MESH)
    pl.semaphore_wait(barrier, len(greeted))

    started = []

    def remote(src, dst, target):
        at = len(started)
        copy = pltpu.make_async_remote_copy(
            src_ref=src,
            dst_ref=dst,
            send_sem=send_sem.at[at],
            recv_sem=recv_sem.at[at],
            device_id=target,
            device_id_type=MESH,
        )
        copy.start()
        started.append(copy)
        return copy

    part = width // (2 * n_grp)
    chunk = part // 2

    def rows_of(g, w, c):
        return pl.ds(pl.multiple_of((g * 2 + w % 2) * part + c * chunk, chunk), chunk)

    def head_out(c):
        rows = rows_of(grp, win, c)
        return [remote(wh_h.at[rows], wh_v.at[seq, rows], dev(grp, win, p)) for p in peers]

    def head_spread(c, arrived):
        rows = rows_of(grp, win, c)
        by_x, by_z = [], []
        for e, copy in enumerate(arrived):
            copy.wait_recv()
            block = wh_v.at[(seq + n - 2 * (e + 1)) % n, rows]
            by_x.append(remote(block, block, across))
            by_z.append(remote(block, block, beside))
        return by_x, by_z

    def head_relay(c, by_x, by_z):
        relayed = []
        for e in range(half - 1):
            shard = (seq + n - 2 * (e + 1)) % n
            if c == 0:
                by_z[e].wait_recv()
                block = wh_v.at[shard, rows_of(grp, other_win, c)]
                relayed.append(remote(block, block, across))
            else:
                by_x[e].wait_recv()
                block = wh_v.at[shard, rows_of(other_grp, win, c)]
                relayed.append(remote(block, block, beside))
        return relayed

    arrive_0 = head_out(0)

    loads["x"].wait()
    normed_v[...] = normalize(x_v[...].astype(jnp.float32)).astype(jnp.bfloat16)
    loads["wk"].wait()
    loads["wv"].wait()
    kv_far, kv_near = [], []
    for p in range(PAIRS):
        kv_v[seq, p, :, :KP] = jnp.dot(
            normed_v[...], wk_v[:, p * KP : (p + 1) * KP], preferred_element_type=jnp.float32
        ).astype(jnp.bfloat16)
        kv_v[seq, p, :, KP:] = jnp.dot(
            normed_v[...], wv_v[:, p * VP : (p + 1) * VP], preferred_element_type=jnp.float32
        ).astype(jnp.bfloat16)
        block = kv_v.at[seq, p]
        kv_far.append([remote(block, block, dev(grp, win, s)) for s in peers])
        kv_near.append([remote(block, block, sibling)])
    arrive_1 = head_out(1)
    own_sib = remote(wh_h, wh_v.at[seq], sibling)
    loads["wq"].wait()
    q_v[...] = jnp.dot(normed_v[...], wq_v[...], preferred_element_type=jnp.float32).astype(
        jnp.bfloat16
    )
    loads["skip"].wait()
    for j in range(width // 128):
        wide_v[j] = skip_v[:, j * 128 : (j + 1) * 128].astype(jnp.float32)

    def kv_relay(p):
        for e in range(half - 1):
            kv_far[p][e].wait_recv()
            block = kv_v.at[(seq + n - 2 * (e + 1)) % n, p]
            kv_near[p].append(remote(block, block, sibling))

    def attend(p):
        for copy in kv_near[p]:
            copy.wait_recv()
        keys = kv_v[:, p, :, :KP].reshape(n * tok, KP)
        vals = kv_v[:, p, :, KP:].reshape(n * tok, VP)
        pair = q_v[:, p * KP : (p + 1) * KP]
        key_lane = lax.broadcasted_iota(jnp.int32, (tok, KP), 1)
        outs = []
        for h in range(2):
            mine = key_lane < KEY if h == 0 else key_lane >= KEY
            masked = jnp.where(mine, pair.astype(jnp.float32), 0.0).astype(jnp.bfloat16)
            scores = lax.dot_general(
                masked, keys, (((1,), (1,)), ((), ())), preferred_element_type=jnp.float32
            ) * (1.0 / math.sqrt(KEY))
            expo = jnp.exp(scores - jnp.max(scores, axis=-1, keepdims=True))
            denom = jnp.sum(expo, axis=-1, keepdims=True)
            outs.append(
                jnp.dot(expo.astype(jnp.bfloat16), vals, preferred_element_type=jnp.float32) / denom
            )
        val_lane = lax.broadcasted_iota(jnp.int32, (tok, VP), 1)
        att_v[:, p * VP : (p + 1) * VP] = jnp.where(val_lane < VAL, outs[0], outs[1]).astype(
            jnp.bfloat16
        )

    kv_relay(0)
    x_0, z_0 = head_spread(0, arrive_0)
    attend(0)
    for p in range(1, PAIRS):
        kv_relay(p)
        attend(p)
    relay_0 = head_relay(0, x_0, z_0)
    loads["wo"].wait()

    def up_step(t, carry):
        at = pl.ds(pl.multiple_of(t * TILE, TILE), TILE)
        resid = x_v[:, at].astype(jnp.float32) + jnp.dot(
            att_v[...], wo_v[:, at], preferred_element_type=jnp.float32
        )
        for m in range(2):
            here = pl.ds(pl.multiple_of(t * TILE + m * 128, 128), 128)
            mine = resid[:, m * 128 : (m + 1) * 128]
            even = (mine + wide_v[t * (TILE // 128) + m, pl.ds(0, tok, stride=2), :]).astype(jnp.bfloat16)
            odd = (mine + wide_v[t * (TILE // 128) + m, pl.ds(1, tok, stride=2), :]).astype(jnp.bfloat16)
            even = even.astype(jnp.float32)
            odd = odd.astype(jnp.float32)
            even_v[:, here] = even
            odd_v[:, here] = odd
            halo_s[0, :, here] = even[:8]
            halo_s[1, :, here] = odd[tok - 8 :]
        return carry

    lax.fori_loop(0, width // TILE, up_step, 0)
    to_prev = remote(halo_s.at[0], halo_r.at[0], dev(grp, win, (seq + n - 1) % n))
    to_next = remote(halo_s.at[1], halo_r.at[1], dev(grp, win, (seq + 1) % n))
    x_1, z_1 = head_spread(1, arrive_1)
    loads["taps"].wait()
    to_prev.wait_recv()
    to_next.wait_recv()

    def conv_step(t, carry):
        at = pl.ds(pl.multiple_of(t * 128, 128), 128)
        even = even_v[:, at]
        odd = odd_v[:, at]
        row = lax.broadcasted_iota(jnp.int32, (tok, 128), 0)
        before = jnp.where(seq == 0, 0.0, halo_r[1, 7:8, at])
        after = jnp.where(seq == n - 1, 0.0, halo_r[0, 0:1, at])
        odd_prev = jnp.where(row == 0, before, pltpu.roll(odd, 1, axis=0))
        even_next = jnp.where(row == tok - 1, after, pltpu.roll(even, tok - 1, axis=0))
        t0, t1, t2 = taps_v[0:1, at], taps_v[1:2, at], taps_v[2:3, at]
        first = t0 * odd_prev + t1 * even + t2 * odd
        second = t0 * even + t1 * odd + t2 * even_next
        wide_v[t, pl.ds(0, tok, stride=2), :] = gelu(first)
        wide_v[t, pl.ds(1, tok, stride=2), :] = gelu(second)
        return carry

    lax.fori_loop(0, width // 128, conv_step, 0)
    for k in range(n):
        for j in range(width // 128):
            feat_v[k, :, j * 128 : (j + 1) * 128] = wide_v[
                j, k * piece : (k + 1) * piece, :
            ].astype(jnp.bfloat16)

    ahead = seq // half
    to_win = (win + ahead) % n_win

    def feature_copy(d):
        owner = (seq + d) % n
        return pltpu.make_async_remote_copy(
            src_ref=feat_v.at[owner],
            dst_ref=got_v.at[seq],
            send_sem=fsend_sem.at[d],
            recv_sem=frecv_sem.at[d],
            device_id=dev(grp, to_win, owner),
            device_id_type=MESH,
        )

    feats = [feature_copy(d) for d in range(n)]
    for d in list(range(half, n)) + list(range(1, half)):
        feats[d].start()

    @pl.when(seq >= half)
    def _():
        feats[0].start()

    @pl.when(seq < half)
    def _():
        got_v[seq] = feat_v[seq]

    relay_1 = head_relay(1, x_1, z_1)
    late = []
    loads["wh"].wait()
    for e in range(half - 1):
        x_0[e].wait_recv()
        relay_0[e].wait_recv()
        z_1[e].wait_recv()
        relay_1[e].wait_recv()
        shard = wh_v.at[(seq + n - 2 * (e + 1)) % n]
        late.append(remote(shard, shard, sibling))
    loads["bias"].wait()

    for d in range(1, n):
        feats[d].wait_recv()

    @pl.when(seq >= half)
    def _():
        feats[0].wait_recv()

    def blend_step(t, carry):
        at = pl.ds(pl.multiple_of(t * 128, 128), 128)
        blocks = []
        for i in range(half):
            place = lax.broadcasted_iota(jnp.int32, (piece, 128), 0) + (i * n + seq) * piece
            place = place.astype(jnp.float32)
            blocks.append(
                (
                    (place + 1.0) * got_v[i, :, at].astype(jnp.float32)
                    + (window_len - place) * got_v[half + i, :, at].astype(jnp.float32)
                )
                * (1.0 / (window_len + 1.0))
            )
        blend_v[:, at] = jnp.concatenate(blocks, axis=0).astype(jnp.bfloat16)
        return carry

    lax.fori_loop(0, width // 128, blend_step, 0)

    def apply_head(shard):
        def head_step(t, carry):
            at = pl.ds(pl.multiple_of(t * TILE, TILE), TILE)
            base = pl.ds(pl.multiple_of(shard * cols + t * TILE, TILE), TILE)
            z = (
                jnp.dot(blend_v[...], wh_v[shard, :, at], preferred_element_type=jnp.float32)
                + bias_v[:, base]
            )
            z = jnp.maximum(z, 0.0) + jnp.log1p(jnp.exp(-jnp.abs(z)))
            for i in range(half):
                out_v[i, :, base] = z[i * piece : (i + 1) * piece].astype(jnp.bfloat16)
            return carry

        lax.fori_loop(0, cols // TILE, head_step, 0)

    stores = []

    def store(shard):
        base = pl.ds(pl.multiple_of(shard * cols, cols), cols)
        at = len(stores)
        stores.append(
            pltpu.make_async_copy(out_v.at[:, :, base], out_h.at[:, :, base], store_sem.at[at])
        )
        stores[at].start()

    apply_head(seq)
    store(seq)
    own_sib.wait_recv()
    apply_head(sib_seq)
    store(sib_seq)
    for e in range(half - 1):
        shard = (seq + n - 2 * (e + 1)) % n
        apply_head(shard)
        store(shard)
    for e in range(half - 1):
        late[e].wait_recv()
        shard = (sib_seq + n - 2 * (e + 1)) % n
        apply_head(shard)
        store(shard)

    for copy in stores:
        copy.wait()
    for copy in started:
        copy.wait_send()
    for d in range(1, n):
        feats[d].wait_send()

    @pl.when(seq >= half)
    def _():
        feats[0].wait_send()


def local(embeddings, skip_rows, w_query, w_key, w_value, w_out, conv_taps, w_head, head_bias):
    n = lax.axis_size("seq")
    n_win = lax.axis_size("win")
    n_grp = lax.axis_size("grp")
    _, tok, width = embeddings.shape
    cols = w_head.shape[1]
    piece = 2 * tok // n
    half = n // 2
    others = half - 1
    copies = PAIRS * (2 * others + 1) + 1 + 9 * others + 2
    bf16, f32 = jnp.bfloat16, jnp.float32
    dma = pltpu.SemaphoreType.DMA
    tracks = pl.pallas_call(
        functools.partial(kernel, n, n_win, n_grp),
        out_shape=jax.ShapeDtypeStruct((half, piece, n * cols), bf16),
        in_specs=[pl.BlockSpec(memory_space=pl.ANY)] * 9,
        out_specs=pl.BlockSpec(memory_space=pl.ANY),
        scratch_shapes=[
            pltpu.VMEM((tok, width), bf16),
            pltpu.VMEM((2 * tok, width), bf16),
            pltpu.VMEM(w_query.shape, bf16),
            pltpu.VMEM(w_key.shape, bf16),
            pltpu.VMEM(w_value.shape, bf16),
            pltpu.VMEM(w_out.shape, bf16),
            pltpu.VMEM(conv_taps.shape, f32),
            pltpu.VMEM((1, n * cols), f32),
            pltpu.VMEM((n, width, cols), bf16),
            pltpu.VMEM((tok, width), bf16),
            pltpu.VMEM((tok, HEADS * KEY), bf16),
            pltpu.VMEM((n, PAIRS, tok, KP + VP), bf16),
            pltpu.VMEM((tok, HEADS * VAL), bf16),
            pltpu.VMEM((width // 128, 2 * tok, 128), f32),
            pltpu.VMEM((tok, width), f32),
            pltpu.VMEM((tok, width), f32),
            pltpu.VMEM((2, 8, width), f32),
            pltpu.VMEM((2, 8, width), f32),
            pltpu.VMEM((n, piece, width), bf16),
            pltpu.VMEM((n, piece, width), bf16),
            pltpu.VMEM((tok, width), bf16),
            pltpu.VMEM((half, piece, n * cols), bf16),
            dma((9,)),
            dma((copies,)),
            dma((copies,)),
            dma((n,)),
            dma((n,)),
            dma((n,)),
        ],
        compiler_params=pltpu.CompilerParams(
            collective_id=0, has_side_effects=True, vmem_limit_bytes=60 * 1024 * 1024
        ),
    )(
        embeddings, skip_rows, w_query, w_key, w_value, w_out, conv_taps, w_head,
        head_bias.reshape(1, -1),
    )
    return tracks[None, :, None]


def solution(mesh):
    return jax.shard_map(
        local,
        mesh=mesh,
        in_specs=(
            P(("grp", "win"), "seq", None),
            P(("grp", "win"), "seq", None),
            P(),
            P(),
            P(),
            P(),
            P(),
            P(None, "seq"),
            P(),
        ),
        out_specs=P(("grp", "win"), None, "seq", None, None),
        check_vma=False,
    )
```

time: 149 us -> 86.3 us (0.58)
  the two profiles are of different devices: /device:TPU:0 before, /device:TPU:7 now
where the time goes in v1:
time: 86.3 us; the launch traced here: 86.2 us
  Pallas kernels  83.4 us (97%)
  local copies, waits for them, and re-layouts  2.7 us (3%)
    pallas_call x1, Pallas kernels, local(): pl.pallas_call(functools.partial(kernel, n, n_win, n_grp), out_shape=jax....  83.4 us
    unnamed x1, local copies, waits for them, and re-layouts  2.7 us

profile of v1, /device:TPU:7, one launch (start us, length us, event | category | flops | bytes accessed | tf_op | source)
XLA Modules:
  0.0 86.2 jit_solution(3992821189036526994)
XLA Ops:
  0.0 83.4 %shard_map.91 = bf16[2,96,4096]{2,1,0:T(8,128)(2,1)} custom-call(bf16[1,192,1536]{2,1,0:T(8,128)(2,1)} %emb_h.1, bf16[1,384,1536]{2,1,0:T(8,128)(2,1)} %skip_h.1, bf16[1536,256]{1,0:T(8,128)(2,1)} %wq_h.1, bf16[1536,256]{1,0:T(8,128)(2,1)} %wk_h.1, bf16[1536,768]{1,0:T(8,128)(2,1)} %wv_h.1, bf16[768,1536]{1,0:T(8,128)(2,1)} %wo_h.1, f32[3,1536]{1,0:T(4,128)} %taps_h.1, ...), custom_call_target="tpu_custom_call" | custom-call | tf_op jit(solution)/shard_map/pallas_call | solution.py:379
  83.5 2.7 %copy.12 = bf16[1,2,1,96,4096]{4,3,2,1,0:T(8,128)(2,1)} copy(bf16[1,2,1,96,4096]{4,3,2,1,0:T(8,128)(2,1)} %bitcast.4) | data formatting | bytes 3145728

commit v2 on v1

--- a/solution.py
+++ b/solution.py
@@ -15,6 +15,7 @@
 KP = 2 * KEY
 VP = 2 * VAL
 TILE = 256
+CHUNKS = 4
 MESH = pl.DeviceIdType.MESH
 
 
@@ -34,8 +35,8 @@
     emb_h, skip_h, wq_h, wk_h, wv_h, wo_h, taps_h, wh_h, bias_h, out_h,
     x_v, skip_v, wq_v, wk_v, wv_v, wo_v, taps_v, bias_v, wh_v,
     normed_v, q_v, kv_v, att_v, wide_v, even_v, odd_v, halo_s, halo_r,
-    feat_v, got_v, blend_v, out_v,
-    load_sem, send_sem, recv_sem, fsend_sem, frecv_sem, store_sem,
+    feat_v, mid_v, got_v, blend_v, out_v,
+    load_sem, send_sem, recv_sem, fsend_sem, frecv_sem, bsend_sem, brecv_sem, store_sem,
 ):
     grp = lax.axis_index("grp")
     win = lax.axis_index("win")
@@ -101,7 +102,7 @@
         return copy
 
     part = width // (2 * n_grp)
-    chunk = part // 2
+    chunk = part // CHUNKS
 
     def rows_of(g, w, c):
         return pl.ds(pl.multiple_of((g * 2 + w % 2) * part + c * chunk, chunk), chunk)
@@ -110,31 +111,48 @@
         rows = rows_of(grp, win, c)
         return [remote(wh_h.at[rows], wh_v.at[seq, rows], dev(grp, win, p)) for p in peers]
 
-    def head_spread(c, arrived):
+    arrived = set()
+
+    def arrive(copy):
+        if id(copy) not in arrived:
+            arrived.add(id(copy))
+            copy.wait_recv()
+
+    far_shards = [(seq + n - 2 * e) % n for e in range(1, half)]
+    y_in, x_in, z_in, diag_in = {}, {}, {}, {}
+
+    def head_spread(c):
         rows = rows_of(grp, win, c)
-        by_x, by_z = [], []
-        for e, copy in enumerate(arrived):
-            copy.wait_recv()
-            block = wh_v.at[(seq + n - 2 * (e + 1)) % n, rows]
-            by_x.append(remote(block, block, across))
-            by_z.append(remote(block, block, beside))
-        return by_x, by_z
-
-    def head_relay(c, by_x, by_z):
-        relayed = []
-        for e in range(half - 1):
-            shard = (seq + n - 2 * (e + 1)) % n
-            if c == 0:
-                by_z[e].wait_recv()
+        x_in[c], z_in[c] = [], []
+        for copy, shard in zip(y_in[c], far_shards):
+            arrive(copy)
+            block = wh_v.at[shard, rows]
+            x_in[c].append(remote(block, block, across))
+            z_in[c].append(remote(block, block, beside))
+
+    def head_relay(c):
+        diag_in[c] = []
+        for e, shard in enumerate(far_shards):
+            if c % 2 == 0:
+                arrive(z_in[c][e])
                 block = wh_v.at[shard, rows_of(grp, other_win, c)]
-                relayed.append(remote(block, block, across))
+                diag_in[c].append(remote(block, block, across))
             else:
-                by_x[e].wait_recv()
+                arrive(x_in[c][e])
                 block = wh_v.at[shard, rows_of(other_grp, win, c)]
-                relayed.append(remote(block, block, beside))
-        return relayed
-
-    arrive_0 = head_out(0)
+                diag_in[c].append(remote(block, block, beside))
+
+    late = [[] for _ in far_shards]
+
+    def head_share(copies, g, w):
+        for e, shard in enumerate(far_shards):
+            for c in range(CHUNKS):
+                arrive(copies[c][e])
+            at = pl.ds(pl.multiple_of((g * 2 + w % 2) * part, part), part)
+            block = wh_v.at[shard, at]
+            late[e].append(remote(block, block, sibling))
+
+    y_in[0] = head_out(0)
 
     loads["x"].wait()
     normed_v[...] = normalize(x_v[...].astype(jnp.float32)).astype(jnp.bfloat16)
@@ -151,8 +169,8 @@
         block = kv_v.at[seq, p]
         kv_far.append([remote(block, block, dev(grp, win, s)) for s in peers])
         kv_near.append([remote(block, block, sibling)])
-    arrive_1 = head_out(1)
-    own_sib = remote(wh_h, wh_v.at[seq], sibling)
+    for c in range(1, CHUNKS):
+        y_in[c] = head_out(c)
     loads["wq"].wait()
     q_v[...] = jnp.dot(normed_v[...], wq_v[...], preferred_element_type=jnp.float32).astype(
         jnp.bfloat16
@@ -192,12 +210,14 @@
         )
 
     kv_relay(0)
-    x_0, z_0 = head_spread(0, arrive_0)
+    head_spread(0)
     attend(0)
     for p in range(1, PAIRS):
         kv_relay(p)
         attend(p)
-    relay_0 = head_relay(0, x_0, z_0)
+    head_spread(1)
+    head_relay(0)
+    own_sib = remote(wh_h, wh_v.at[seq], sibling)
     loads["wo"].wait()
 
     def up_step(t, carry):
@@ -221,7 +241,7 @@
     lax.fori_loop(0, width // TILE, up_step, 0)
     to_prev = remote(halo_s.at[0], halo_r.at[0], dev(grp, win, (seq + n - 1) % n))
     to_next = remote(halo_s.at[1], halo_r.at[1], dev(grp, win, (seq + 1) % n))
-    x_1, z_1 = head_spread(1, arrive_1)
+    head_spread(2)
     loads["taps"].wait()
     to_prev.wait_recv()
     to_next.wait_recv()
@@ -249,50 +269,82 @@
                 j, k * piece : (k + 1) * piece, :
             ].astype(jnp.bfloat16)
 
-    ahead = seq // half
-    to_win = (win + ahead) % n_win
-
-    def feature_copy(d):
+    feats = []
+    for d in list(range(half, n)) + list(range(1, half)):
         owner = (seq + d) % n
-        return pltpu.make_async_remote_copy(
-            src_ref=feat_v.at[owner],
-            dst_ref=got_v.at[seq],
-            send_sem=fsend_sem.at[d],
-            recv_sem=frecv_sem.at[d],
-            device_id=dev(grp, to_win, owner),
+        feats.append(
+            pltpu.make_async_remote_copy(
+                src_ref=feat_v.at[owner],
+                dst_ref=mid_v.at[seq],
+                send_sem=fsend_sem.at[d],
+                recv_sem=frecv_sem.at[seq],
+                device_id=dev(grp, win, owner),
+                device_id_type=MESH,
+            )
+        )
+        feats[-1].start()
+    mid_v[seq] = feat_v[seq]
+
+    def feature_wait(slot):
+        pltpu.make_async_remote_copy(
+            src_ref=feat_v.at[slot],
+            dst_ref=mid_v.at[slot],
+            send_sem=fsend_sem.at[0],
+            recv_sem=frecv_sem.at[slot],
+            device_id=dev(grp, win, slot),
             device_id_type=MESH,
-        )
-
-    feats = [feature_copy(d) for d in range(n)]
-    for d in list(range(half, n)) + list(range(1, half)):
-        feats[d].start()
-
-    @pl.when(seq >= half)
-    def _():
-        feats[0].start()
-
-    @pl.when(seq < half)
-    def _():
-        got_v[seq] = feat_v[seq]
-
-    relay_1 = head_relay(1, x_1, z_1)
-    late = []
+        ).wait_recv()
+
+    behind = []
+
+    def feature_forward(i):
+        at = (seq + i) % half
+        if i == 0:
+
+            @pl.when(seq < half)
+            def _():
+                feature_wait(half + at)
+
+        else:
+            feature_wait(half + at)
+        behind.append(
+            pltpu.make_async_remote_copy(
+                src_ref=mid_v.at[half + at],
+                dst_ref=got_v.at[at],
+                send_sem=bsend_sem.at[i],
+                recv_sem=brecv_sem.at[i],
+                device_id=dev(grp, next_win, seq),
+                device_id_type=MESH,
+            )
+        )
+        behind[-1].start()
+
+    head_spread(3)
+    head_share(y_in, grp, win)
+    head_relay(1)
+    head_relay(2)
+    feature_forward(0)
+    head_relay(3)
+    for i in range(1, half):
+        feature_forward(i)
     loads["wh"].wait()
-    for e in range(half - 1):
-        x_0[e].wait_recv()
-        relay_0[e].wait_recv()
-        z_1[e].wait_recv()
-        relay_1[e].wait_recv()
-        shard = wh_v.at[(seq + n - 2 * (e + 1)) % n]
-        late.append(remote(shard, shard, sibling))
+    head_share(x_in, other_grp, win)
+    head_share(z_in, grp, other_win)
+    head_share(diag_in, other_grp, other_win)
     loads["bias"].wait()
 
-    for d in range(1, n):
-        feats[d].wait_recv()
-
-    @pl.when(seq >= half)
-    def _():
-        feats[0].wait_recv()
+    for i in range(half):
+        at = (seq + i) % half
+        if i == 0:
+
+            @pl.when(seq >= half)
+            def _():
+                feature_wait(at)
+
+        else:
+            feature_wait(at)
+    for copy in behind:
+        copy.wait_recv()
 
     def blend_step(t, carry):
         at = pl.ds(pl.multiple_of(t * 128, 128), 128)
@@ -302,8 +354,8 @@
             place = place.astype(jnp.float32)
             blocks.append(
                 (
-                    (place + 1.0) * got_v[i, :, at].astype(jnp.float32)
-                    + (window_len - place) * got_v[half + i, :, at].astype(jnp.float32)
+                    (place + 1.0) * mid_v[i, :, at].astype(jnp.float32)
+                    + (window_len - place) * got_v[i, :, at].astype(jnp.float32)
                 )
                 * (1.0 / (window_len + 1.0))
             )
@@ -347,7 +399,8 @@
         apply_head(shard)
         store(shard)
     for e in range(half - 1):
-        late[e].wait_recv()
+        for copy in late[e]:
+            copy.wait_recv()
         shard = (sib_seq + n - 2 * (e + 1)) % n
         apply_head(shard)
         store(shard)
@@ -356,12 +409,8 @@
         copy.wait()
     for copy in started:
         copy.wait_send()
-    for d in range(1, n):
-        feats[d].wait_send()
-
-    @pl.when(seq >= half)
-    def _():
-        feats[0].wait_send()
+    for copy in feats + behind:
+        copy.wait_send()
 
 
 def local(embeddings, skip_rows, w_query, w_key, w_value, w_out, conv_taps, w_head, head_bias):
@@ -373,7 +422,7 @@
     piece = 2 * tok // n
     half = n // 2
     others = half - 1
-    copies = PAIRS * (2 * others + 1) + 1 + 9 * others + 2
+    copies = PAIRS * (2 * others + 1) + 1 + (4 * CHUNKS + 4) * others + 2
     bf16, f32 = jnp.bfloat16, jnp.float32
     dma = pltpu.SemaphoreType.DMA
     tracks = pl.pallas_call(
@@ -402,6 +451,7 @@
             pltpu.VMEM((2, 8, width), f32),
             pltpu.VMEM((n, piece, width), bf16),
             pltpu.VMEM((n, piece, width), bf16),
+            pltpu.VMEM((half, piece, width), bf16),
             pltpu.VMEM((tok, width), bf16),
             pltpu.VMEM((half, piece, n * cols), bf16),
             dma((9,)),
@@ -409,6 +459,8 @@
             dma((copies,)),
             dma((n,)),
             dma((n,)),
+            dma((half,)),
+            dma((half,)),
             dma((n,)),
         ],
         compiler_params=pltpu.CompilerParams(

time: 86.3 us -> 74.2 us (0.86)
  the two profiles are of different devices: /device:TPU:7 before, /device:TPU:0 now
where the time goes in v2:
time: 74.2 us; the launch traced here: 74.1 us
  Pallas kernels  71.4 us (96%)
  local copies, waits for them, and re-layouts  2.7 us (4%)
    pallas_call x1, Pallas kernels, local(): pl.pallas_call(functools.partial(kernel, n, n_win, n_grp), out_shape=jax....  71.4 us
    unnamed x1, local copies, waits for them, and re-layouts  2.7 us

profile of v2, /device:TPU:0, one launch (start us, length us, event | category | flops | bytes accessed | tf_op | source)
XLA Modules:
  0.0 74.1 jit_solution(17930375606306768866)
XLA Ops:
  0.0 71.4 %shard_map.91 = bf16[2,96,4096]{2,1,0:T(8,128)(2,1)} custom-call(bf16[1,192,1536]{2,1,0:T(8,128)(2,1)} %emb_h.1, bf16[1,384,1536]{2,1,0:T(8,128)(2,1)} %skip_h.1, bf16[1536,256]{1,0:T(8,128)(2,1)} %wq_h.1, bf16[1536,256]{1,0:T(8,128)(2,1)} %wk_h.1, bf16[1536,768]{1,0:T(8,128)(2,1)} %wv_h.1, bf16[768,1536]{1,0:T(8,128)(2,1)} %wo_h.1, f32[3,1536]{1,0:T(4,128)} %taps_h.1, ...), custom_call_target="tpu_custom_call" | custom-call | tf_op jit(solution)/shard_map/pallas_call | solution.py:428
  71.4 2.7 %copy.12 = bf16[1,2,1,96,4096]{4,3,2,1,0:T(8,128)(2,1)} copy(bf16[1,2,1,96,4096]{4,3,2,1,0:T(8,128)(2,1)} %bitcast.4) | data formatting | bytes 3145728

commit v3 on v2

--- a/solution.py
+++ b/solution.py
@@ -16,6 +16,7 @@
 VP = 2 * VAL
 TILE = 256
 CHUNKS = 4
+BANDS = 4
 MESH = pl.DeviceIdType.MESH
 
 
@@ -169,8 +170,7 @@
         block = kv_v.at[seq, p]
         kv_far.append([remote(block, block, dev(grp, win, s)) for s in peers])
         kv_near.append([remote(block, block, sibling)])
-    for c in range(1, CHUNKS):
-        y_in[c] = head_out(c)
+    y_in[1] = head_out(1)
     loads["wq"].wait()
     q_v[...] = jnp.dot(normed_v[...], wq_v[...], preferred_element_type=jnp.float32).astype(
         jnp.bfloat16
@@ -241,7 +241,8 @@
     lax.fori_loop(0, width // TILE, up_step, 0)
     to_prev = remote(halo_s.at[0], halo_r.at[0], dev(grp, win, (seq + n - 1) % n))
     to_next = remote(halo_s.at[1], halo_r.at[1], dev(grp, win, (seq + 1) % n))
-    head_spread(2)
+    for c in range(2, CHUNKS):
+        y_in[c] = head_out(c)
     loads["taps"].wait()
     to_prev.wait_recv()
     to_next.wait_recv()
@@ -262,71 +263,80 @@
         wide_v[t, pl.ds(1, tok, stride=2), :] = gelu(second)
         return carry
 
-    lax.fori_loop(0, width // 128, conv_step, 0)
-    for k in range(n):
-        for j in range(width // 128):
-            feat_v[k, :, j * 128 : (j + 1) * 128] = wide_v[
-                j, k * piece : (k + 1) * piece, :
-            ].astype(jnp.bfloat16)
-
+    band = width // BANDS
+    lanes = band // 128
     feats = []
-    for d in list(range(half, n)) + list(range(1, half)):
-        owner = (seq + d) % n
-        feats.append(
-            pltpu.make_async_remote_copy(
-                src_ref=feat_v.at[owner],
-                dst_ref=mid_v.at[seq],
-                send_sem=fsend_sem.at[d],
-                recv_sem=frecv_sem.at[seq],
-                device_id=dev(grp, win, owner),
-                device_id_type=MESH,
+    for b in range(BANDS):
+        lax.fori_loop(b * lanes, (b + 1) * lanes, conv_step, 0)
+        for k in range(n):
+            for j in range(b * lanes, (b + 1) * lanes):
+                feat_v[k, :, j * 128 : (j + 1) * 128] = wide_v[
+                    j, k * piece : (k + 1) * piece, :
+                ].astype(jnp.bfloat16)
+        span = pl.ds(b * band, band)
+        for d in list(range(half, n)) + list(range(1, half)):
+            owner = (seq + d) % n
+            feats.append(
+                pltpu.make_async_remote_copy(
+                    src_ref=feat_v.at[owner, :, span],
+                    dst_ref=mid_v.at[seq, :, span],
+                    send_sem=fsend_sem.at[d, b],
+                    recv_sem=frecv_sem.at[seq, b],
+                    device_id=dev(grp, win, owner),
+                    device_id_type=MESH,
+                )
             )
-        )
-        feats[-1].start()
-    mid_v[seq] = feat_v[seq]
-
-    def feature_wait(slot):
+            feats[-1].start()
+        mid_v[seq, :, span] = feat_v[seq, :, span]
+        if b == 1:
+            head_spread(2)
+
+    def feature_wait(slot, b):
+        span = pl.ds(b * band, band)
         pltpu.make_async_remote_copy(
-            src_ref=feat_v.at[slot],
-            dst_ref=mid_v.at[slot],
-            send_sem=fsend_sem.at[0],
-            recv_sem=frecv_sem.at[slot],
+            src_ref=feat_v.at[slot, :, span],
+            dst_ref=mid_v.at[slot, :, span],
+            send_sem=fsend_sem.at[0, b],
+            recv_sem=frecv_sem.at[slot, b],
             device_id=dev(grp, win, slot),
             device_id_type=MESH,
         ).wait_recv()
 
     behind = []
 
-    def feature_forward(i):
-        at = (seq + i) % half
-        if i == 0:
-
-            @pl.when(seq < half)
-            def _():
-                feature_wait(half + at)
-
-        else:
-            feature_wait(half + at)
-        behind.append(
-            pltpu.make_async_remote_copy(
-                src_ref=mid_v.at[half + at],
-                dst_ref=got_v.at[at],
-                send_sem=bsend_sem.at[i],
-                recv_sem=brecv_sem.at[i],
-                device_id=dev(grp, next_win, seq),
-                device_id_type=MESH,
+    def feature_forward(b):
+        span = pl.ds(b * band, band)
+        for i in range(half):
+            at = (seq + i) % half
+            if i == 0:
+
+                @pl.when(seq < half)
+                def _():
+                    feature_wait(half + at, b)
+
+            else:
+                feature_wait(half + at, b)
+            behind.append(
+                pltpu.make_async_remote_copy(
+                    src_ref=mid_v.at[half + at, :, span],
+                    dst_ref=got_v.at[at, :, span],
+                    send_sem=bsend_sem.at[i, b],
+                    recv_sem=brecv_sem.at[i, b],
+                    device_id=dev(grp, next_win, seq),
+                    device_id_type=MESH,
+                )
             )
-        )
-        behind[-1].start()
-
+            behind[-1].start()
+
+    head_relay(1)
     head_spread(3)
+    feature_forward(0)
+    head_relay(2)
+    feature_forward(1)
+    head_relay(3)
+    for b in range(2, BANDS):
+        feature_forward(b)
     head_share(y_in, grp, win)
-    head_relay(1)
-    head_relay(2)
-    feature_forward(0)
-    head_relay(3)
-    for i in range(1, half):
-        feature_forward(i)
     loads["wh"].wait()
     head_share(x_in, other_grp, win)
     head_share(z_in, grp, other_win)
@@ -335,14 +345,15 @@
 
     for i in range(half):
         at = (seq + i) % half
-        if i == 0:
-
-            @pl.when(seq >= half)
-            def _():
-                feature_wait(at)
-
-        else:
-            feature_wait(at)
+        for b in range(BANDS):
+            if i == 0:
+
+                @pl.when(seq >= half)
+                def _():
+                    feature_wait(at, b)
+
+            else:
+                feature_wait(at, b)
     for copy in behind:
         copy.wait_recv()
 
@@ -457,10 +468,10 @@
             dma((9,)),
             dma((copies,)),
             dma((copies,)),
-            dma((n,)),
-            dma((n,)),
-            dma((half,)),
-            dma((half,)),
+            dma((n, BANDS)),
+            dma((n, BANDS)),
+            dma((half, BANDS)),
+            dma((half, BANDS)),
             dma((n,)),
         ],
         compiler_params=pltpu.CompilerParams(

time: 74.2 us -> 75.5 us (1.018)
  Pallas kernels: 71.4 us -> 72.6 us
    pallas_call x1, Pallas kernels: 71.4 us -> 72.6 us  [local(): pl.pallas_call(functools.partial(kernel, n, n_win, n_grp), out_shape=jax....]
where the time goes in v3:
time: 75.5 us; the launch traced here: 75.3 us
  Pallas kernels  72.6 us (96%)
  local copies, waits for them, and re-layouts  2.7 us (4%)
    pallas_call x1, Pallas kernels, local(): pl.pallas_call(functools.partial(kernel, n, n_win, n_grp), out_shape=jax....  72.6 us
    unnamed x1, local copies, waits for them, and re-layouts  2.7 us

profile of v3, /device:TPU:0, one launch (start us, length us, event | category | flops | bytes accessed | tf_op | source)
XLA Modules:
  0.0 75.3 jit_solution(2891785197040300500)
XLA Ops:
  0.0 72.6 %shard_map.91 = bf16[2,96,4096]{2,1,0:T(8,128)(2,1)} custom-call(bf16[1,192,1536]{2,1,0:T(8,128)(2,1)} %emb_h.1, bf16[1,384,1536]{2,1,0:T(8,128)(2,1)} %skip_h.1, bf16[1536,256]{1,0:T(8,128)(2,1)} %wq_h.1, bf16[1536,256]{1,0:T(8,128)(2,1)} %wk_h.1, bf16[1536,768]{1,0:T(8,128)(2,1)} %wv_h.1, bf16[768,1536]{1,0:T(8,128)(2,1)} %wo_h.1, f32[3,1536]{1,0:T(4,128)} %taps_h.1, ...), custom_call_target="tpu_custom_call" | custom-call | tf_op jit(solution)/shard_map/pallas_call | solution.py:439
  72.6 2.7 %copy.12 = bf16[1,2,1,96,4096]{4,3,2,1,0:T(8,128)(2,1)} copy(bf16[1,2,1,96,4096]{4,3,2,1,0:T(8,128)(2,1)} %bitcast.4) | data formatting | bytes 3145728

commit v4 on v3

--- a/solution.py
+++ b/solution.py
@@ -170,7 +170,8 @@
         block = kv_v.at[seq, p]
         kv_far.append([remote(block, block, dev(grp, win, s)) for s in peers])
         kv_near.append([remote(block, block, sibling)])
-    y_in[1] = head_out(1)
+    for c in range(1, CHUNKS):
+        y_in[c] = head_out(c)
     loads["wq"].wait()
     q_v[...] = jnp.dot(normed_v[...], wq_v[...], preferred_element_type=jnp.float32).astype(
         jnp.bfloat16
@@ -241,8 +242,7 @@
     lax.fori_loop(0, width // TILE, up_step, 0)
     to_prev = remote(halo_s.at[0], halo_r.at[0], dev(grp, win, (seq + n - 1) % n))
     to_next = remote(halo_s.at[1], halo_r.at[1], dev(grp, win, (seq + 1) % n))
-    for c in range(2, CHUNKS):
-        y_in[c] = head_out(c)
+    head_spread(2)
     loads["taps"].wait()
     to_prev.wait_recv()
     to_next.wait_recv()
@@ -289,7 +289,7 @@
             feats[-1].start()
         mid_v[seq, :, span] = feat_v[seq, :, span]
         if b == 1:
-            head_spread(2)
+            head_spread(3)
 
     def feature_wait(slot, b):
         span = pl.ds(b * band, band)
@@ -329,11 +329,10 @@
             behind[-1].start()
 
     head_relay(1)
-    head_spread(3)
+    head_relay(2)
     feature_forward(0)
-    head_relay(2)
+    head_relay(3)
     feature_forward(1)
-    head_relay(3)
     for b in range(2, BANDS):
         feature_forward(b)
     head_share(y_in, grp, win)

time: 75.5 us -> 73 us (0.967)
  Pallas kernels: 72.6 us -> 70.1 us
    pallas_call x1, Pallas kernels: 72.6 us -> 70.1 us  [local(): pl.pallas_call(functools.partial(kernel, n, n_win, n_grp), out_shape=jax....]
where the time goes in v4:
time: 73 us; the launch traced here: 72.9 us
  Pallas kernels  70.1 us (96%)
  local copies, waits for them, and re-layouts  2.7 us (4%)
    pallas_call x1, Pallas kernels, local(): pl.pallas_call(functools.partial(kernel, n, n_win, n_grp), out_shape=jax....  70.1 us
    unnamed x1, local copies, waits for them, and re-layouts  2.7 us

profile of v4, /device:TPU:0, one launch (start us, length us, event | category | flops | bytes accessed | tf_op | source)
XLA Modules:
  0.0 72.9 jit_solution(10470974115804759036)
XLA Ops:
  0.0 70.1 %shard_map.91 = bf16[2,96,4096]{2,1,0:T(8,128)(2,1)} custom-call(bf16[1,192,1536]{2,1,0:T(8,128)(2,1)} %emb_h.1, bf16[1,384,1536]{2,1,0:T(8,128)(2,1)} %skip_h.1, bf16[1536,256]{1,0:T(8,128)(2,1)} %wq_h.1, bf16[1536,256]{1,0:T(8,128)(2,1)} %wk_h.1, bf16[1536,768]{1,0:T(8,128)(2,1)} %wv_h.1, bf16[768,1536]{1,0:T(8,128)(2,1)} %wo_h.1, f32[3,1536]{1,0:T(4,128)} %taps_h.1, ...), custom_call_target="tpu_custom_call" | custom-call | tf_op jit(solution)/shard_map/pallas_call | solution.py:438
  70.1 2.7 %copy.12 = bf16[1,2,1,96,4096]{4,3,2,1,0:T(8,128)(2,1)} copy(bf16[1,2,1,96,4096]{4,3,2,1,0:T(8,128)(2,1)} %bitcast.4) | data formatting | bytes 3145728
